TPU v7x, 32 devices: a whole 2x2x4 slice. The times are simulated.
32 devices in a mesh: wide: 16 (over z, y, x), narrow: 2 (over core).
Axes of the slice: x: 2, y: 2, z: 4, core: 2. Of those that a mesh axis runs over, the one named last changes fastest.
Arguments:
- x_trial: float32 [2, 512, 512], P(None, 'wide', 'narrow'), may hold values from -6 to 6
- psi_orb: float32 [512, 16384], P('narrow', 'wide'), may hold values from -0.046875 to 0.046875
- phi_orb: float32 [512, 16384], P('wide', 'narrow'), may hold values from -0.046875 to 0.046875
- screened: float32 [16384, 16384], P('wide', 'narrow'), may hold values from -192 to 192
- eps_val: float32 [512], P('wide'), may hold values from -1 to -0.1
- eps_cond: float32 [512], P('narrow'), may hold values from 0.1 to 1
Outputs:
- applied: float32 [2, 512, 512], P(None, 'wide', 'narrow')
All inputs are finite; a program needn't handle non-finite values.
Results may differ from a plain program's by a relative error of at most 0.00011.
Values sent between devices are 32-bit elements; how exact they have to be, the bound alone decides.
A program may use at most 192 MiB of HBM per device.

v0:
```python
import jax
import jax.numpy as jnp
from jax import lax
from jax.sharding import PartitionSpec as P


def local(x_trial, psi_orb, phi_orb, screened, eps_val, eps_cond):
    precise = lax.Precision.HIGHEST
    psi_rows = lax.all_gather(psi_orb, "narrow", axis=0, tiled=True)
    phi_cols = lax.all_gather(phi_orb, "wide", axis=0, tiled=True)
    x_cols = lax.all_gather(x_trial, "narrow", axis=2, tiled=True)
    x_whole = lax.all_gather(x_cols, "wide", axis=1, tiled=True)
    half_map = jnp.einsum("vr,tvc->trc", psi_rows, x_whole, precision=precise)
    pair_tile = jnp.einsum("trc,cs->trs", half_map, phi_cols, precision=precise) * screened[None]
    back_map = jnp.einsum("trs,cs->trc", pair_tile, phi_cols, precision=precise)
    summed = lax.psum_scatter(back_map, "narrow", scatter_dimension=2, tiled=True)
    val_part = jnp.einsum("vr,trc->tvc", psi_rows, summed, precision=precise)
    kernel = lax.psum_scatter(val_part, "wide", scatter_dimension=1, tiled=True)
    energy_gap = eps_cond[None, None, :] - eps_val[None, :, None]
    return kernel + energy_gap * x_trial


def solution(mesh):
    placed = (
        P(None, "wide", "narrow"),
        P("narrow", "wide"),
        P("wide", "narrow"),
        P("wide", "narrow"),
        P("wide"),
        P("narrow"),
    )
    return jax.shard_map(
        local, mesh=mesh, in_specs=placed, out_specs=P(None, "wide", "narrow"), check_vma=False
    )
```

profile of v0, /device:TPU:0, one launch (start us, length us, event | category | flops | bytes accessed | tf_op | source)
XLA Modules:
  0.0 646.4 jit_solution(13201375299929367361)
XLA Ops:
  6.5 0.7 all-gather.6.cloned.1.call-update
  7.3 0.0 all-gather.4.cloned.1.call-start
  7.3 3.7 all_gather.12
  11.0 0.0 all-gather.4.cloned.1.call-update
  11.0 0.0 all-gather.8.cloned.1.call-start
  11.1 0.7 all-gather.8.cloned.1.call-update
  11.8 0.0 reduce-scatter.2.cloned.1.call-start
  11.8 10.4 %all-gather.6.cloned.1.call-done = f32[512,1024]{1,0:T(8,128)} async-done(((f32[256,1024]{1,0:T(8,128)}), f32[512,1024]{1,0:T(8,128)}) %all-gather.6.cloned.1.call-update) | async-done | bytes 2097168 | tf_op jit(solution)/shard_map/all_gather | solution.py:9
  22.2 64.3 %all-gather.4.cloned.1.call-done = f32[2,512,512]{2,1,0:T(8,128)} async-done(((f32[2,32,512]{2,1,0:T(8,128)}), f32[2,512,512]{2,1,0:T(8,128)}) %all-gather.4.cloned.1.call-update) | async-done | bytes 2097168 | tf_op jit(solution)/shard_map/all_gather | solution.py:12
  86.5 10.3 %fusion.9 = f32[2,512,1024]{2,1,0:T(8,128)} fusion(f32[2,512,512]{2,1,0:T(8,128)} %all-gather.4.cloned.1.call-done, f32[512,1024]{1,0:T(8,128)} %all-gather.6.cloned.1.call-done), kind=kOutput, calls=%fused_computation.9 | convolution fusion | flops 6442450944 | bytes 8388608 | tf_op jit(solution)/shard_map/vr,tvc->trc/dot_general | solution.py:13
  96.8 182.3 %all-gather.8.cloned.1.call-done = f32[512,8192]{1,0:T(8,128)} async-done(((f32[32,8192]{1,0:T(8,128)}), f32[512,8192]{1,0:T(8,128)}) %all-gather.8.cloned.1.call-update) | async-done | bytes 16777232 | tf_op jit(solution)/shard_map/all_gather | solution.py:10
  279.0 112.7 %fusion.4 = f32[2,1024,8192]{2,1,0:T(8,128)} fusion(f32[512,8192]{1,0:T(8,128)} %all-gather.8.cloned.1.call-done, f32[2,512,1024]{2,1,0:T(8,128)} %fusion.9), kind=kOutput, calls=%fused_computation.4 | convolution fusion | flops 103079215104 | bytes 88080384 | tf_op jit(solution)/shard_map/trc,cs->trs/dot_general | solution.py:14
  391.8 112.9 %fusion = f32[2,1024,512]{2,1,0:T(8,128)} fusion(f32[2,1024,8192]{2,1,0:T(8,128)} %fusion.4, f32[1024,8192]{1,0:T(8,128)} %param.9, f32[512,8192]{1,0:T(8,128)} %all-gather.8.cloned.1.call-done), kind=kOutput, calls=%fused_computation | convolution fusion | flops 103095992320 | bytes 121634816 | tf_op jit(solution)/shard_map/trs,cs->trc/dot_general | solution.py:15
  504.7 0.0 reduce-scatter.2.cloned.1.call-update
  504.8 0.3 all-reduce.3.cloned.1.call-start
  505.1 9.9 %reduce-scatter.2.cloned.1.call-done = f32[2,1024,256]{2,1,0:T(8,128)} async-done(((f32[2,1024,512]{2,1,0:T(8,128)}), f32[2,1024,256]{2,1,0:T(8,128)}) %reduce-scatter.2.cloned.1.call-update) | async-done | bytes 2097168 | tf_op jit(solution)/shard_map/reduce_scatter | solution.py:16
  514.9 8.3 %fusion.11 = f32[2,512,256]{1,2,0:T(8,128)S(1)} fusion(f32[2,1024,256]{2,1,0:T(8,128)} %reduce-scatter.2.cloned.1.call-done, f32[512,1024]{1,0:T(8,128)S(1)} %copy-done), kind=kOutput, calls=%fused_computation.11 | convolution fusion | flops 3221225472 | bytes 5242880 | tf_op jit(solution)/shard_map/vr,trc->tvc/dot_general | solution.py:17
  523.2 1.3 copy.14
  524.5 0.0 all-reduce.3.cloned.1.call-update
  524.6 0.6 dynamic-slice
  525.8 0.1 broadcast_subtract_fusion
  525.9 112.5 %all-reduce.3.cloned.1.call-done = f32[2,512,256]{2,0,1:T(2,128)} async-done(((f32[2,512,256]{2,0,1:T(2,128)}), f32[2,512,256]{2,0,1:T(2,128)}) %all-reduce.3.cloned.1.call-update) | async-done | bytes 1048592
  638.4 0.8 constant_dynamic-slice_fusion
  639.2 0.6 copy_add_fusion
  (11 shorter events, 0.0 us)
Async XLA Ops:
  6.5 15.7 %all-gather.6.cloned.1.call-start = ((), (), s32[]{:S(2)}) async-start(), calls=%async_computation.2 | async-start | bytes 3145728 | tf_op jit(solution)/shard_map/all_gather | solution.py:9
  7.3 79.2 %all-gather.4.cloned.1.call-start = ((), (), s32[]{:S(2)}) async-start(), calls=%async_computation.1 | async-start | bytes 2228224 | tf_op jit(solution)/shard_map/all_gather | solution.py:12
  11.0 268.0 %all-gather.8.cloned.1.call-start = ((), (), s32[]{:S(2)}) async-start(), calls=%async_computation.3 | async-start | bytes 17825792 | tf_op jit(solution)/shard_map/all_gather | solution.py:10
  11.8 503.1 %reduce-scatter.2.cloned.1.call-start = ((), (), s32[]{:S(2)}) async-start(), calls=%async_computation.4 | async-start | bytes 6291456 | tf_op jit(solution)/shard_map/reduce_scatter | solution.py:16
  504.7 10.2 %copy-start = (f32[512,1024]{1,0:T(8,128)S(1)}, f32[512,1024]{1,0:T(8,128)}, u32[]{:S(2)}) copy-start(f32[512,1024]{1,0:T(8,128)} %all-gather.6.cloned.1.call-done) | copy-start | bytes 6291460
  504.7 19.9 %copy-start.4 = (u32[32]{0:T(128)S(1)}, u32[32]{0:T(128)}, u32[]{:S(2)}) copy-start(u32[32]{0:T(128)} %constant.2) | copy-start | bytes 388
  504.7 21.1 %copy-start.2 = (f32[256]{0:T(256)S(1)}, f32[256]{0:T(256)}, u32[]{:S(2)}) copy-start(f32[256]{0:T(256)} %param.11) | copy-start | bytes 3076
  504.7 21.1 %copy-start.3 = (f32[32]{0:T(128)S(1)}, f32[32]{0:T(128)}, u32[]{:S(2)}) copy-start(f32[32]{0:T(128)} %param.10) | copy-start | bytes 388
  504.7 134.5 %copy-start.1 = (f32[2,32,256]{2,1,0:T(8,128)S(1)}, f32[2,32,256]{2,1,0:T(8,128)}, u32[]{:S(2)}) copy-start(f32[2,32,256]{2,1,0:T(8,128)} %param.6) | copy-start | bytes 196612
  504.8 133.6 %all-reduce.3.cloned.1.call-start = ((), (), s32[]{:S(2)}) async-start(), calls=%async_computation.5 | async-start | bytes 2097152
Sparse Core Ops, SparseCore 0:
  8.9 13.2 all-gather.5
  25.0 61.4 all-gather.3
  89.3 189.7 all-gather.7
  504.8 10.0 reduce-scatter.1
  524.7 113.6 all-reduce.2
where the time goes:
time: 647 us; the launch traced here: 646 us
  waiting for transfers between devices  381 us (59%)
  matrix products  244 us (38%)
  between operations  13.9 us (2%)
    all_gather x1, waiting for transfers between devices, local(): phi_cols = lax.all_gather(phi_orb, 'wide', axis=0, tiled=True)  182 us
    unnamed x6, waiting for transfers between devices  114 us
    dot_general x1, matrix products, local(): back_map = jnp.einsum('trs,cs->trc', pair_tile, phi_cols, precision=precise)  113 us
    dot_general x1, matrix products, local(): jnp.einsum('trc,cs->trs', half_map, phi_cols, precision=precise)  113 us
    all_gather x1, waiting for transfers between devices, local(): x_whole = lax.all_gather(x_cols, 'wide', axis=1, tiled=True)  64.3 us
  transfers between devices with their start and end apart: 5, of which 5 were waited for; matrix products, arithmetic and copies ran while one was open for 2% of the time, Pallas kernels for 0%

commit v1 on v0

--- a/solution.py
+++ b/solution.py
@@ -9,8 +9,38 @@
     psi_rows = lax.all_gather(psi_orb, "narrow", axis=0, tiled=True)
     phi_cols = lax.all_gather(phi_orb, "wide", axis=0, tiled=True)
     x_cols = lax.all_gather(x_trial, "narrow", axis=2, tiled=True)
-    x_whole = lax.all_gather(x_cols, "wide", axis=1, tiled=True)
-    half_map = jnp.einsum("vr,tvc->trc", psi_rows, x_whole, precision=precise)
+    size, place, rows = (lax.axis_size("wide"), lax.axis_index("wide"), x_cols.shape[1])
+    ahead = [(i, (i + 1) % size) for i in range(size)]
+    left = [(i, (i - 1) % size) for i in range(size)]
+    halfway = size // 2
+    from_left = from_right = x_cols
+    total = jnp.einsum(
+        "vr,tvc->trc",
+        lax.dynamic_slice_in_dim(psi_rows, place * rows, x_cols.shape[1], axis=0),
+        x_cols,
+        precision=precise,
+    )
+    for turn in range(1, halfway + 1):
+        from_left = lax.ppermute(from_left, "wide", ahead)
+        if turn < size - halfway:
+            from_right = lax.ppermute(from_right, "wide", left)
+            total = total + jnp.einsum(
+                "vr,tvc->trc",
+                lax.dynamic_slice_in_dim(
+                    psi_rows, (place + turn) % size * rows, from_right.shape[1], axis=0
+                ),
+                from_right,
+                precision=precise,
+            )
+        total = total + jnp.einsum(
+            "vr,tvc->trc",
+            lax.dynamic_slice_in_dim(
+                psi_rows, (place - turn) % size * rows, from_left.shape[1], axis=0
+            ),
+            from_left,
+            precision=precise,
+        )
+    half_map = total
     pair_tile = jnp.einsum("trc,cs->trs", half_map, phi_cols, precision=precise) * screened[None]
     back_map = jnp.einsum("trs,cs->trc", pair_tile, phi_cols, precision=precise)
     summed = lax.psum_scatter(back_map, "narrow", scatter_dimension=2, tiled=True)

time: 647 us -> 633 us (0.978); the launches traced: 646 us -> 624 us
  waiting for transfers between devices: 381 us -> 215 us
  matrix products: 244 us -> 345 us
  starting transfers between devices: 0.42 us -> 43 us
    all_gather x1, waiting for transfers between devices: 182 us -> 59.3 us  [local(): phi_cols = lax.all_gather(phi_orb, 'wide', axis=0, tiled=True)]
    dot_general x1 -> x16, matrix products: 10.3 us -> 84.2 us  [the longest x8 42.7 us: local(): jnp.einsum('vr,tvc->trc', lax.dynamic_slice_in_dim(psi_rows, (place - tur...]
    all_gather x1 -> x0, waiting for transfers between devices: 64.3 us -> none  [local(): x_whole = lax.all_gather(x_cols, 'wide', axis=1, tiled=True)]
    ppermute x0 -> x15, starting transfers between devices: none -> 42.6 us  [the longest x7 39.7 us: local(): from_right = lax.ppermute(from_right, 'wide', left)]
    ppermute x0 -> x15, waiting for transfers between devices: none -> 32.2 us  [the longest x8 24.6 us: local(): from_left = lax.ppermute(from_left, 'wide', ahead)]
    dot_general x1, matrix products: 113 us -> 140 us  [local(): jnp.einsum('trc,cs->trs', half_map, phi_cols, precision=precise)]
    all_gather x1, waiting for transfers between devices: 10.4 us -> 0.02 us  [local(): psi_rows = lax.all_gather(psi_orb, 'narrow', axis=0, tiled=True)]
    unnamed x6 -> x5, waiting for transfers between devices: 114 us -> 114 us
  transfers between devices with their start and end apart: 5 -> 19, of which waited for: 5 -> 14; matrix products, arithmetic and copies ran while one was open for 2% -> 14% of each run, Pallas kernels for 0% -> 0%
where the time goes in v1:
time: 633 us; the launch traced here: 624 us
  matrix products  345 us (55%)
  waiting for transfers between devices  215 us (34%)
  starting transfers between devices  43 us (7%)
  between operations  14.4 us (2%)
    dot_general x1, matrix products, local(): jnp.einsum('trc,cs->trs', half_map, phi_cols, precision=precise)  140 us
    unnamed x5, waiting for transfers between devices  114 us
    dot_general x1, matrix products, local(): back_map = jnp.einsum('trs,cs->trc', pair_tile, phi_cols, precision=precise)  113 us
    all_gather x1, waiting for transfers between devices, local(): phi_cols = lax.all_gather(phi_orb, 'wide', axis=0, tiled=True)  59.3 us
    dot_general x8, matrix products, local(): jnp.einsum('vr,tvc->trc', lax.dynamic_slice_in_dim(psi_rows, (place - tur...  42.7 us
    ppermute x7, starting transfers between devices, local(): from_right = lax.ppermute(from_right, 'wide', left)  39.7 us
    dot_general x7, matrix products, local(): jnp.einsum('vr,tvc->trc', lax.dynamic_slice_in_dim(psi_rows, (place + tur...  36.5 us
    ppermute x8, waiting for transfers between devices, local(): from_left = lax.ppermute(from_left, 'wide', ahead)  24.6 us
  transfers between devices with their start and end apart: 19, of which 14 were waited for; matrix products, arithmetic and copies ran while one was open for 14% of the time, Pallas kernels for 0%

profile of v1, /device:TPU:0, one launch (start us, length us, event | category | flops | bytes accessed | tf_op | source)
XLA Modules:
  0.0 623.6 jit_solution(12701375967152622295)
XLA Ops:
  21.0 5.6 collective-permute-start.2
  29.6 5.6 collective-permute-start.4
  40.4 6.1 collective-permute-start.6
  52.1 6.1 collective-permute-start.8
  64.3 6.1 collective-permute-start.10
  73.2 6.1 collective-permute-start.12
  79.3 5.7 collective-permute-done.13
  85.1 6.1 fusion.29
  91.2 5.1 fusion.33
  101.4 5.1 fusion.37
  106.5 5.1 fusion.39
  111.7 5.1 fusion.41
  116.7 5.1 fusion.43
  121.8 5.1 fusion.45
  126.9 5.3 fusion.47
  142.3 5.1 fusion.53
  157.4 5.9 fusion.31
  163.4 6.0 fusion.27
  169.4 59.3 %all-gather.5.cloned.1.call-done = f32[512,8192]{1,0:T(8,128)} async-done(((f32[32,8192]{1,0:T(8,128)}), f32[512,8192]{1,0:T(8,128)}) %all-gather.5.cloned.1.call-update) | async-done | bytes 16777232 | tf_op jit(solution)/shard_map/all_gather | solution.py:10
  228.6 139.6 %fusion.4 = f32[2,1024,8192]{2,1,0:T(8,128)} fusion(f32[512,8192]{1,0:T(8,128)} %all-gather.5.cloned.1.call-done, f32[1024,2,512]{2,0,1:T(8,128)} %fusion.27, f32[1024,2,512]{2,0,1:T(8,128)} %fusion.29, f32[1024,2,512]{2,0,1:T(8,128)} %fusion.31, f32[1024,2,512]{2,0,1:T(8,128)} %fusion.33, f32[1024,2,512]{2,0,1:T(8,128)} %fusion.35, ...), kind=kOutput, calls=%fused_computation.4 | convolution fusion | flops 103094943744 | bytes 150994944 | tf_op jit(solution)/shard_map/trc,cs->trs/dot_general | solution.py:44
  368.2 113.1 %fusion = f32[2,1024,512]{2,1,0:T(8,128)} fusion(f32[2,1024,8192]{2,1,0:T(8,128)} %fusion.4, f32[1024,8192]{1,0:T(8,128)} %param.9, f32[512,8192]{1,0:T(8,128)} %all-gather.5.cloned.1.call-done), kind=kOutput, calls=%fused_computation | convolution fusion | flops 103095992320 | bytes 121634816 | tf_op jit(solution)/shard_map/trs,cs->trc/dot_general | solution.py:45
  481.8 9.8 %reduce-scatter.2.cloned.1.call-done = f32[2,1024,256]{2,1,0:T(8,128)} async-done(((f32[2,1024,512]{2,1,0:T(8,128)}), f32[2,1024,256]{2,1,0:T(8,128)}) %reduce-scatter.2.cloned.1.call-update) | async-done | bytes 2097168 | tf_op jit(solution)/shard_map/reduce_scatter | solution.py:46
  491.6 8.3 %fusion.24 = f32[2,512,256]{1,2,0:T(8,128)S(1)} fusion(f32[2,1024,256]{2,1,0:T(8,128)} %reduce-scatter.2.cloned.1.call-done, f32[512,1024]{1,0:T(8,128)S(1)} %copy-done), kind=kOutput, calls=%fused_computation.24 | convolution fusion | flops 3221225472 | bytes 5242880 | tf_op jit(solution)/shard_map/vr,trc->tvc/dot_general | solution.py:47
  502.6 112.5 %all-reduce.3.cloned.1.call-done = f32[2,512,256]{2,0,1:T(2,128)} async-done(((f32[2,512,256]{2,0,1:T(2,128)}), f32[2,512,256]{2,0,1:T(2,128)}) %all-reduce.3.cloned.1.call-update) | async-done | bytes 1048592
  (65 shorter events, 66.2 us)
Async XLA Ops:
  6.5 78.5 %all-gather.3.cloned.1.call-start = ((), (), s32[]{:S(2)}) async-start(), calls=%async_computation.1 | async-start | bytes 3145728 | tf_op jit(solution)/shard_map/all_gather | solution.py:9
  7.3 221.4 %all-gather.5.cloned.1.call-start = ((), (), s32[]{:S(2)}) async-start(), calls=%async_computation.2 | async-start | bytes 17825792 | tf_op jit(solution)/shard_map/all_gather | solution.py:10
  8.0 483.6 %reduce-scatter.2.cloned.1.call-start = ((), (), s32[]{:S(2)}) async-start(), calls=%async_computation.3 | async-start | bytes 6291456 | tf_op jit(solution)/shard_map/reduce_scatter | solution.py:46
  10.3 10.7 %collective-permute-start.1 = (f32[2,32,512]{2,1,0:T(8,128)S(1)}, f32[2,32,512]{2,1,0:T(8,128)S(1)}, u32[]{:S(2)}, u32[]{:S(2)}) collective-permute-start(f32[2,32,512]{2,1,0:T(8,128)S(1)} %all_gather.10), channel_id=1, source_target_pairs={{0,2},{2,4},{4,6},{6,8},{8,10},{10,12},{12,14},{14,16},{16,18},{18... | collective-permute-start | bytes 393224 | tf_op jit(solution)/shard_map/ppermute | solution.py:24
  13.1 7.9 %collective-permute-start = (f32[2,32,512]{2,1,0:T(8,128)S(1)}, f32[2,32,512]{2,1,0:T(8,128)S(1)}, u32[]{:S(2)}, u32[]{:S(2)}) collective-permute-start(f32[2,32,512]{2,1,0:T(8,128)S(1)} %all_gather.10), channel_id=1, source_target_pairs={{0,30},{2,0},{4,2},{6,4},{8,6},{10,8},{12,10},{14,12},{16,14},{18,... | collective-permute-start | bytes 393224 | tf_op jit(solution)/shard_map/ppermute | solution.py:26
  21.0 8.6 %collective-permute-start.3 = (f32[2,32,512]{2,1,0:T(8,128)S(1)}, f32[2,32,512]{2,1,0:T(8,128)S(1)}, u32[]{:S(2)}, u32[]{:S(2)}) collective-permute-start(f32[2,32,512]{2,1,0:T(8,128)S(1)} %collective-permute-done.1), channel_id=1, source_target_pairs={{0,2},{2,4},{4,6},{6,8},{8,10},{10,12},{12,14},{14,16},{16,18},{18... | collective-permute-start | bytes 393224 | tf_op jit(solution)/shard_map/ppermute | solution.py:24
  21.0 8.6 %collective-permute-start.2 = (f32[2,32,512]{2,1,0:T(8,128)S(1)}, f32[2,32,512]{2,1,0:T(8,128)S(1)}, u32[]{:S(2)}, u32[]{:S(2)}) collective-permute-start(f32[2,32,512]{2,1,0:T(8,128)S(1)} %collective-permute-done), channel_id=1, source_target_pairs={{0,30},{2,0},{4,2},{6,4},{8,6},{10,8},{12,10},{14,12},{16,14},{18,... | collective-permute-start | bytes 393224 | tf_op jit(solution)/shard_map/ppermute | solution.py:26
  29.6 8.7 %collective-permute-start.5 = (f32[2,32,512]{2,1,0:T(8,128)S(1)}, f32[2,32,512]{2,1,0:T(8,128)S(1)}, u32[]{:S(2)}, u32[]{:S(2)}) collective-permute-start(f32[2,32,512]{2,1,0:T(8,128)S(1)} %collective-permute-done.3), channel_id=1, source_target_pairs={{0,2},{2,4},{4,6},{6,8},{8,10},{10,12},{12,14},{14,16},{16,18},{18... | collective-permute-start | bytes 393224 | tf_op jit(solution)/shard_map/ppermute | solution.py:24
  29.6 10.8 %collective-permute-start.4 = (f32[2,32,512]{2,1,0:T(8,128)S(1)}, f32[2,32,512]{2,1,0:T(8,128)S(1)}, u32[]{:S(2)}, u32[]{:S(2)}) collective-permute-start(f32[2,32,512]{2,1,0:T(8,128)S(1)} %collective-permute-done.2), channel_id=1, source_target_pairs={{0,30},{2,0},{4,2},{6,4},{8,6},{10,8},{12,10},{14,12},{16,14},{18,... | collective-permute-start | bytes 393224 | tf_op jit(solution)/shard_map/ppermute | solution.py:26
  38.3 11.5 %collective-permute-start.7 = (f32[2,32,512]{2,1,0:T(8,128)S(1)}, f32[2,32,512]{2,1,0:T(8,128)S(1)}, u32[]{:S(2)}, u32[]{:S(2)}) collective-permute-start(f32[2,32,512]{2,1,0:T(8,128)S(1)} %collective-permute-done.5), channel_id=1, source_target_pairs={{0,2},{2,4},{4,6},{6,8},{8,10},{10,12},{12,14},{14,16},{16,18},{18... | collective-permute-start | bytes 393224 | tf_op jit(solution)/shard_map/ppermute | solution.py:24
  40.4 11.7 %collective-permute-start.6 = (f32[2,32,512]{2,1,0:T(8,128)S(1)}, f32[2,32,512]{2,1,0:T(8,128)S(1)}, u32[]{:S(2)}, u32[]{:S(2)}) collective-permute-start(f32[2,32,512]{2,1,0:T(8,128)S(1)} %collective-permute-done.4), channel_id=1, source_target_pairs={{0,30},{2,0},{4,2},{6,4},{8,6},{10,8},{12,10},{14,12},{16,14},{18,... | collective-permute-start | bytes 393224 | tf_op jit(solution)/shard_map/ppermute | solution.py:26
  49.8 11.5 %collective-permute-start.9 = (f32[2,32,512]{2,1,0:T(8,128)S(1)}, f32[2,32,512]{2,1,0:T(8,128)S(1)}, u32[]{:S(2)}, u32[]{:S(2)}) collective-permute-start(f32[2,32,512]{2,1,0:T(8,128)S(1)} %collective-permute-done.7), channel_id=1, source_target_pairs={{0,2},{2,4},{4,6},{6,8},{8,10},{10,12},{12,14},{14,16},{16,18},{18... | collective-permute-start | bytes 393224 | tf_op jit(solution)/shard_map/ppermute | solution.py:24
  52.1 12.2 %collective-permute-start.8 = (f32[2,32,512]{2,1,0:T(8,128)S(1)}, f32[2,32,512]{2,1,0:T(8,128)S(1)}, u32[]{:S(2)}, u32[]{:S(2)}) collective-permute-start(f32[2,32,512]{2,1,0:T(8,128)S(1)} %collective-permute-done.6), channel_id=1, source_target_pairs={{0,30},{2,0},{4,2},{6,4},{8,6},{10,8},{12,10},{14,12},{16,14},{18,... | collective-permute-start | bytes 393224 | tf_op jit(solution)/shard_map/ppermute | solution.py:26
  61.3 11.6 %collective-permute-start.11 = (f32[2,32,512]{2,1,0:T(8,128)S(1)}, f32[2,32,512]{2,1,0:T(8,128)S(1)}, u32[]{:S(2)}, u32[]{:S(2)}) collective-permute-start(f32[2,32,512]{2,1,0:T(8,128)S(1)} %collective-permute-done.9), channel_id=1, source_target_pairs={{0,2},{2,4},{4,6},{6,8},{8,10},{10,12},{12,14},{14,16},{16,18},{18... | collective-permute-start | bytes 393224 | tf_op jit(solution)/shard_map/ppermute | solution.py:24
  64.3 20.8 %copy-start.4 = (f32[2,32,512]{2,1,0:T(8,128)}, f32[2,32,512]{2,1,0:T(8,128)S(1)}, u32[]{:S(2)}) copy-start(f32[2,32,512]{2,1,0:T(8,128)S(1)} %collective-permute-done.8) | copy-start | bytes 393220
  64.3 8.9 %collective-permute-start.10 = (f32[2,32,512]{2,1,0:T(8,128)S(1)}, f32[2,32,512]{2,1,0:T(8,128)S(1)}, u32[]{:S(2)}, u32[]{:S(2)}) collective-permute-start(f32[2,32,512]{2,1,0:T(8,128)S(1)} %collective-permute-done.8), channel_id=1, source_target_pairs={{0,30},{2,0},{4,2},{6,4},{8,6},{10,8},{12,10},{14,12},{16,14},{18,... | collective-permute-start | bytes 393224 | tf_op jit(solution)/shard_map/ppermute | solution.py:26
  72.9 12.1 %collective-permute-start.13 = (f32[2,32,512]{2,1,0:T(8,128)S(1)}, f32[2,32,512]{2,1,0:T(8,128)S(1)}, u32[]{:S(2)}, u32[]{:S(2)}) collective-permute-start(f32[2,32,512]{2,1,0:T(8,128)S(1)} %collective-permute-done.11), channel_id=1, source_target_pairs={{0,2},{2,4},{4,6},{6,8},{8,10},{10,12},{12,14},{14,16},{16,18},{18... | collective-permute-start | bytes 393224 | tf_op jit(solution)/shard_map/ppermute | solution.py:24
  73.2 84.3 %collective-permute-start.12 = (f32[2,32,512]{2,1,0:T(8,128)S(1)}, f32[2,32,512]{2,1,0:T(8,128)}, u32[]{:S(2)}, u32[]{:S(2)}) collective-permute-start(f32[2,32,512]{2,1,0:T(8,128)S(1)} %collective-permute-done.10), channel_id=1, source_target_pairs={{0,30},{2,0},{4,2},{6,4},{8,6},{10,8},{12,10},{14,12},{16,14},{18,... | collective-permute-start | bytes 393224 | tf_op jit(solution)/shard_map/ppermute | solution.py:26
  85.0 78.3 %collective-permute-start.14 = (f32[2,32,512]{2,1,0:T(8,128)S(1)}, f32[2,32,512]{2,1,0:T(8,128)}, u32[]{:S(2)}, u32[]{:S(2)}) collective-permute-start(f32[2,32,512]{2,1,0:T(8,128)S(1)} %collective-permute-done.13), channel_id=1, source_target_pairs={{0,2},{2,4},{4,6},{6,8},{8,10},{10,12},{12,14},{14,16},{16,18},{18... | collective-permute-start | bytes 393224 | tf_op jit(solution)/shard_map/ppermute | solution.py:24
  481.4 19.8 %copy-start.10 = (u32[32]{0:T(128)S(1)}, u32[32]{0:T(128)}, u32[]{:S(2)}) copy-start(u32[32]{0:T(128)} %constant.113) | copy-start | bytes 388
  481.4 21.1 %copy-start.8 = (f32[256]{0:T(256)S(1)}, f32[256]{0:T(256)}, u32[]{:S(2)}) copy-start(f32[256]{0:T(256)} %param.11) | copy-start | bytes 3076
  481.4 21.1 %copy-start.9 = (f32[32]{0:T(128)S(1)}, f32[32]{0:T(128)}, u32[]{:S(2)}) copy-start(f32[32]{0:T(128)} %param.10) | copy-start | bytes 388
  481.5 134.5 %copy-start.1 = (f32[2,32,256]{2,1,0:T(8,128)S(1)}, f32[2,32,256]{2,1,0:T(8,128)}, u32[]{:S(2)}) copy-start(f32[2,32,256]{2,1,0:T(8,128)} %param.6) | copy-start | bytes 196612
  481.5 133.6 %all-reduce.3.cloned.1.call-start = ((), (), s32[]{:S(2)}) async-start(), calls=%async_computation.4 | async-start | bytes 2097152
  (6 other events, 53.8 us)
Sparse Core Ops, SparseCore 0:
  8.9 13.2 all-gather.2
  25.0 203.6 all-gather.4
  481.5 10.0 reduce-scatter.1
  501.4 113.6 all-reduce.2
